TPU v7x, 256 devices: a whole 4x4x8 slice. The times are simulated.
256 devices in a mesh: ctx: 64 (over x, y_hi, z), tp: 4 (over y_lo, core).
Axes of the slice: x: 4, y: 4 (y_hi: 2, y_lo: 2; y = y_hi * 2 + y_lo), z: 8, core: 2. Of those that a mesh axis runs over, the one named last changes fastest.
Arguments:
- queries: bfloat16 [16384, 2048], P('ctx', 'tp'), may hold values from -6 to 6
- keys: bfloat16 [16384, 2048], P('ctx', 'tp'), may hold values from -6 to 6
- values: bfloat16 [16384, 2048], P('ctx', 'tp'), may hold values from -6 to 6
- out_grad: bfloat16 [16384, 4096], P('ctx', 'tp'), may hold values from -6 to 6
- w_out: bfloat16 [2048, 4096], P('tp'), may hold values from -0.09375 to 0.09375
- offsets: int32 [16, 3], P('tp'), may hold values from 0 to 3, as said below
Outputs:
- query_grad: bfloat16 [16384, 2048], P('ctx', 'tp')
- key_grad: bfloat16 [16384, 2048], P('ctx', 'tp')
- value_grad: bfloat16 [16384, 2048], P('ctx', 'tp')
Inputs may be any that keep to these rules, and one draw needn't show every extreme that they name: offsets[h, l] lies between 0 and 2^l - 1.
All inputs are finite; a program needn't handle non-finite values.
Results may differ from a plain program's by a relative error of at most 0.017.
Values may be sent and summed in bfloat16 or wider, within the bound.
No kernel may reach another device: no remote copies, remote signals or barrier semaphores. Data moves between devices by JAX's collectives and lax.ppermute only.
A program may use at most 64 MiB of HBM per device.

v0:
```python
from functools import reduce
import math
import jax
import jax.numpy as jnp
from jax import lax
from jax.sharding import PartitionSpec as P

LEVELS = 3
KEYS_SEG = 1024
NEGATIVE_FILL = -1e30


def for_sending(array):

    def short(part):
        return part.astype(jnp.bfloat16) if part.dtype == jnp.float32 else part

    return jax.tree.map(short, array)


def passed_along(block, axis, distance):
    devices = range(lax.axis_size(axis))
    route = [((i - distance) % len(devices), i) for i in devices]
    return lax.ppermute(block, axis, route)


def pick_table(offset_col, stride):
    return lax.broadcasted_iota(jnp.int32, (stride, offset_col.shape[0]), 0) == offset_col[None, :]


def pack_rows(whole, pick):
    stride = pick.shape[0]
    grouped = whole.reshape((whole.shape[0] // stride, stride) + whole.shape[1:])
    chosen = pick.reshape((1,) + pick.shape + (1,) * (whole.ndim - 2))
    return jnp.sum(jnp.where(chosen, grouped, jnp.zeros((), whole.dtype)), axis=1)


def spread_rows(packed, pick, fill_value):
    stride = pick.shape[0]
    chosen = pick.reshape((1,) + pick.shape + (1,) * (packed.ndim - 2))
    spread = jnp.where(chosen, packed[:, None], jnp.asarray(fill_value, packed.dtype))
    return spread.reshape((packed.shape[0] * stride,) + packed.shape[1:])


def linked_pairs(offset_col, stride, segment, query_start, key_start, row_count):
    tok_rows = row_count * stride
    total_rows = tok_rows * lax.axis_size("ctx")
    rotation = 2 * tok_rows
    lanes = lax.broadcasted_iota(jnp.int32, (row_count,), 0) * stride
    query_pos = (
        query_start + lanes[None, :, None] + offset_col[:, None, None] - rotation
    ) % total_rows
    key_pos = (key_start + lanes[None, None, :] + offset_col[:, None, None] - rotation) % total_rows
    return (query_pos // segment == key_pos // segment) & (key_pos <= query_pos)


def forward_tile(running, query_pack, key_pair, linked, score_scale):
    row_top, row_total, accumulated = running
    scores = (
        jnp.einsum("ahd,bhd->hab", query_pack, key_pair[0], preferred_element_type=jnp.float32)
        * score_scale
    )
    scores = jnp.where(linked, scores, NEGATIVE_FILL)
    new_top = jnp.maximum(row_top, jnp.max(scores, axis=2).T)
    weights = jnp.where(linked, jnp.exp(scores - new_top.T[:, :, None]), 0.0)
    factor = jnp.exp(row_top - new_top)
    row_total = row_total * factor + jnp.sum(weights, axis=2).T
    weights_high = weights.astype(jnp.bfloat16)
    weights_rest = (weights - weights_high.astype(jnp.float32)).astype(jnp.bfloat16)
    product = jnp.einsum(
        "hab,bhd->ahd", weights_high, key_pair[1], preferred_element_type=jnp.float32
    )
    product = product + jnp.einsum(
        "hab,bhd->ahd", weights_rest, key_pair[1], preferred_element_type=jnp.float32
    )
    accumulated = accumulated * factor[:, :, None] + product
    return (new_top, row_total, accumulated)


def tile_grads(query_side, key_pair, linked, score_scale):
    query_pack, grad_pack, log_pack, delta_pack = query_side
    scores = (
        jnp.einsum("ahd,bhd->hab", query_pack, key_pair[0], preferred_element_type=jnp.float32)
        * score_scale
    )
    scores = jnp.where(linked, scores, NEGATIVE_FILL)
    weights = jnp.where(linked, jnp.exp(scores - log_pack.T[:, :, None]), 0.0)
    prob_grad = jnp.einsum(
        "ahd,bhd->hab", grad_pack, key_pair[1], preferred_element_type=jnp.float32
    )
    score_grad = (weights * (prob_grad - delta_pack.T[:, :, None])).astype(jnp.bfloat16)
    return (weights.astype(jnp.bfloat16), score_grad)


def forward_relay(
    running, query_pack, key_pair, offset_col, stride, segment, relay_turns, score_scale
):
    row_count = query_pack.shape[0]
    tok_rows = row_count * stride
    axis_size = lax.axis_size("ctx")
    device_index = lax.axis_index("ctx")
    stored = (
        jnp.zeros((max(relay_turns, 1),) + key_pair[0].shape, key_pair[0].dtype),
        jnp.zeros((max(relay_turns, 1),) + key_pair[1].shape, key_pair[1].dtype),
    )

    def forward_turn_body(turn_num, carried):
        packet, running, stored = carried
        packet = jax.tree.map(
            lambda part, own: part.astype(own.dtype),
            passed_along(for_sending(packet), "ctx", 1),
            packet,
        )
        key_start = (device_index - turn_num) % axis_size * tok_rows
        linked = linked_pairs(
            offset_col, stride, segment, device_index * tok_rows, key_start, row_count
        )
        running = forward_tile(running, query_pack, packet, linked, score_scale)
        return (packet, running, stored)

    packet, running, stored = lax.fori_loop(
        1, relay_turns + 1, forward_turn_body, (key_pair, running, stored)
    )
    return (running, stored)


def keys_pass(query_side, key_pair, offset_col, stride, segment, relay_turns, score_scale):
    query_pack, grad_pack = (query_side[0], query_side[1])
    row_count = query_pack.shape[0]
    tok_rows = row_count * stride
    axis_size = lax.axis_size("ctx")
    device_index = lax.axis_index("ctx")
    own_start = device_index * tok_rows
    weights_low, score_grad = tile_grads(
        query_side,
        key_pair,
        linked_pairs(offset_col, stride, segment, own_start, own_start, row_count),
        score_scale,
    )
    level_q = jnp.einsum(
        "hab,bhd->ahd", score_grad, key_pair[0], preferred_element_type=jnp.float32
    )
    partial_value = (
        jnp.einsum("hab,ahd->bhd", score_grad, query_pack, preferred_element_type=jnp.float32),
        jnp.einsum("hab,ahd->bhd", weights_low, grad_pack, preferred_element_type=jnp.float32),
    )

    def keys_turn_body(turn_num, carried):
        packet, partial_value, level_q = carried
        packet = jax.tree.map(
            lambda part, own: part.astype(own.dtype),
            passed_along(for_sending(packet), "ctx", 1),
            packet,
        )
        partial_value = jax.tree.map(
            lambda part, own: part.astype(own.dtype),
            passed_along(for_sending(partial_value), "ctx", 1),
            partial_value,
        )
        key_start = (device_index - turn_num) % axis_size * tok_rows
        weights_low, score_grad = tile_grads(
            query_side,
            packet,
            linked_pairs(offset_col, stride, segment, own_start, key_start, row_count),
            score_scale,
        )
        level_q = level_q + jnp.einsum(
            "hab,bhd->ahd", score_grad, packet[0], preferred_element_type=jnp.float32
        )
        partial_value = (
            partial_value[0]
            + jnp.einsum(
                "hab,ahd->bhd", score_grad, query_pack, preferred_element_type=jnp.float32
            ),
            partial_value[1]
            + jnp.einsum(
                "hab,ahd->bhd", weights_low, grad_pack, preferred_element_type=jnp.float32
            ),
        )
        return (packet, partial_value, level_q)

    packet, partial_value, level_q = lax.fori_loop(
        1, relay_turns + 1, keys_turn_body, (key_pair, partial_value, level_q)
    )
    partial_value = (
        passed_along(partial_value[0].astype(jnp.bfloat16), "ctx", -relay_turns).astype(
            jnp.float32
        ),
        passed_along(partial_value[1].astype(jnp.bfloat16), "ctx", -relay_turns).astype(
            jnp.float32
        ),
    )
    return (level_q, partial_value[0], partial_value[1])


def local(queries, keys, values, out_grad, w_out, offsets):
    tok_rows = queries.shape[0]
    head_count = offsets.shape[0]
    head_width = queries.shape[1] // head_count
    axis_size = lax.axis_size("ctx")
    device_index = lax.axis_index("ctx")
    keys_seg = KEYS_SEG
    score_scale = 1.0 / math.sqrt(head_width)
    own_start = device_index * tok_rows
    query_rows = queries.reshape(tok_rows, head_count, head_width)
    key_rows = keys.reshape(tok_rows, head_count, head_width)
    value_rows = values.reshape(tok_rows, head_count, head_width)
    grad_out = jnp.einsum(
        "td,fd->tf",
        lax.all_gather(out_grad, "tp", axis=1, tiled=True),
        w_out,
        preferred_element_type=jnp.float32,
    )
    grad_rows = grad_out.astype(jnp.bfloat16).reshape(tok_rows, head_count, head_width)
    level_data = []
    for level_num in range(LEVELS):
        stride = 2**level_num
        segment = min(keys_seg * stride, tok_rows * axis_size)
        row_count = tok_rows // stride
        relay_turns = min(max(segment // tok_rows, 1), axis_size) - 1
        offset_col = offsets[:, level_num]
        pick = pick_table(offset_col, stride)
        query_pack = pack_rows(query_rows, pick)
        key_pair = (pack_rows(key_rows, pick), pack_rows(value_rows, pick))
        running = (
            jnp.full((row_count, head_count), NEGATIVE_FILL, jnp.float32),
            jnp.zeros((row_count, head_count), jnp.float32),
            jnp.zeros((row_count, head_count, head_width), jnp.float32),
        )
        linked = linked_pairs(offset_col, stride, segment, own_start, own_start, row_count)
        running = forward_tile(running, query_pack, key_pair, linked, score_scale)
        running, stored = forward_relay(
            running, query_pack, key_pair, offset_col, stride, segment, relay_turns, score_scale
        )
        level_data.append(
            (stride, segment, relay_turns, offset_col, pick, query_pack, key_pair, running, stored)
        )
    tops = [spread_rows(entry[7][0], entry[4], NEGATIVE_FILL) for entry in level_data]
    row_top = reduce(jnp.maximum, tops)
    row_total = jnp.zeros((tok_rows, head_count), jnp.float32)
    out_sum = jnp.zeros((tok_rows, head_count, head_width), jnp.float32)
    for entry, level_top in zip(level_data, tops):
        factor = jnp.exp(level_top - row_top)
        row_total = row_total + spread_rows(entry[7][1], entry[4], 0.0) * factor
        out_sum = out_sum + spread_rows(entry[7][2], entry[4], 0.0) * factor[:, :, None]
    log_total = row_top + jnp.log(row_total)
    attn_out = out_sum / row_total[:, :, None]
    delta_rows = jnp.sum(grad_rows.astype(jnp.float32) * attn_out, axis=2)
    grad_q = jnp.zeros((tok_rows, head_count, head_width), jnp.float32)
    grad_k = jnp.zeros((tok_rows, head_count, head_width), jnp.float32)
    grad_v = jnp.zeros((tok_rows, head_count, head_width), jnp.float32)
    for (
        stride,
        segment,
        relay_turns,
        offset_col,
        pick,
        query_pack,
        key_pair,
        running,
        stored,
    ) in level_data:
        query_side = (
            query_pack,
            pack_rows(grad_rows, pick),
            pack_rows(log_total, pick),
            pack_rows(delta_rows, pick),
        )
        level_q, level_k, level_v = keys_pass(
            query_side, key_pair, offset_col, stride, segment, relay_turns, score_scale
        )
        grad_q = grad_q + spread_rows(level_q, pick, 0.0)
        grad_k = grad_k + spread_rows(level_k, pick, 0.0)
        grad_v = grad_v + spread_rows(level_v, pick, 0.0)
    flat_width = head_count * head_width
    return (
        (grad_q * score_scale).reshape(tok_rows, flat_width).astype(jnp.bfloat16),
        (grad_k * score_scale).reshape(tok_rows, flat_width).astype(jnp.bfloat16),
        grad_v.reshape(tok_rows, flat_width).astype(jnp.bfloat16),
    )


def solution(mesh):
    return jax.shard_map(
        local,
        mesh=mesh,
        in_specs=(
            P("ctx", "tp"),
            P("ctx", "tp"),
            P("ctx", "tp"),
            P("ctx", "tp"),
            P("tp", None),
            P("tp", None),
        ),
        out_specs=(P("ctx", "tp"), P("ctx", "tp"), P("ctx", "tp")),
        check_vma=False,
    )
```

profile of v0, /device:TPU:8, one launch (start us, length us, event | category | flops | bytes accessed | tf_op | source)
XLA Modules:
  0.0 897.6 jit_solution(7576920657588802797)
XLA Ops:
  20.9 21.8 %all-gather.2.cloned.1.call-done = bf16[256,4096]{1,0:T(8,128)(2,1)} async-done(((bf16[256,1024]{1,0:T(8,128)(2,1)}), bf16[256,4096]{1,0:T(8,128)(2,1)}) %all-gather.2.cloned.1.call-update) | async-done | bytes 2097168 | tf_op jit(solution)/shard_map/all_gather | solution.py:210
  69.5 71.6 %while.144 = (s32[]{:T(128)}, bf16[256,4,128]{2,0,1:T(8,128)(2,1)}, bf16[256,4,128]{2,0,1:T(8,128)(2,1)}, f32[256,4]{0,1:T(4,128)S(1)}, f32[256,4]{0,1:T(4,128)S...) while((s32[]{:T(128)}, bf16[256,4,128]{2,0,1:T(8,128)(2,1)}, ...), condition=%wide.region_5.6_spmd, body=%wide.region_2.5_spmd.sunk | while | flops 208857616 | bytes 10641786 | solution.py:121
  74.0 10.9 %collective-permute-done = bf16[256,4,128]{2,0,1:T(8,128)(2,1)S(1)} collective-permute-done((bf16[256,4,128]{2,0,1:T(8,128)(2,1)}, bf16[256,4,128]{2,0,1:T(8,128)(2,1)S(1)}, u32[]{:S(2)}, u32[]{:S(2)}) %collective-permute-start) | collective-permute-done | bytes 262176 | tf_op jit(solution)/shard_map/while/body/eval_jaxpr/ppermute | solution.py:24
  95.3 14.3 %collective-permute-done = bf16[256,4,128]{2,0,1:T(8,128)(2,1)S(1)} collective-permute-done((bf16[256,4,128]{2,0,1:T(8,128)(2,1)}, bf16[256,4,128]{2,0,1:T(8,128)(2,1)S(1)}, u32[]{:S(2)}, u32[]{:S(2)}) %collective-permute-start) | collective-permute-done | bytes 262176 | tf_op jit(solution)/shard_map/while/body/eval_jaxpr/ppermute | solution.py:24
  119.1 14.3 %collective-permute-done = bf16[256,4,128]{2,0,1:T(8,128)(2,1)S(1)} collective-permute-done((bf16[256,4,128]{2,0,1:T(8,128)(2,1)}, bf16[256,4,128]{2,0,1:T(8,128)(2,1)S(1)}, u32[]{:S(2)}, u32[]{:S(2)}) %collective-permute-start) | collective-permute-done | bytes 262176 | tf_op jit(solution)/shard_map/while/body/eval_jaxpr/ppermute | solution.py:24
  141.9 173.4 %while.146 = (s32[]{:T(128)}, bf16[64,4,128]{2,0,1:T(8,128)(2,1)S(1)}, bf16[64,4,128]{2,0,1:T(8,128)(2,1)S(1)}, f32[64,4]{0,1:T(4,128)S(1)}, f32[64,4]{0,1:T(4,1...) while((s32[]{:T(128)}, ...), condition=%wide.region_23.24_spmd, body=%wide.region_20.23_spmd.sunk | while | flops 13138703 | bytes 1874298 | solution.py:121
  318.2 98.9 %while.145 = (s32[]{:T(128)}, bf16[128,4,128]{2,0,1:T(8,128)(2,1)S(1)}, bf16[128,4,128]{2,0,1:T(8,128)(2,1)S(1)}, f32[128,4]{0,1:T(4,128)S(1)}, f32[128,4]{0,1:T...) while((s32[]{:T(128)}, ...), condition=%wide.region_14.15_spmd, body=%wide.region_11.14_spmd.sunk | while | flops 52327952 | bytes 4272506 | solution.py:121
  319.3 9.8 %collective-permute-done.2 = bf16[128,4,128]{2,0,1:T(8,128)(2,1)S(1)} collective-permute-done((bf16[128,4,128]{2,0,1:T(8,128)(2,1)S(1)}, bf16[128,4,128]{2,0,1:T(8,128)(2,1)S(1)}, u32[]{:S(2)}, u32[]{:S(2)}) %collective-permute-start.2) | collective-permute-done | bytes 131104 | tf_op jit(solution)/shard_map/while/body/eval_jaxpr/ppermute | solution.py:24
  457.5 74.9 %while.147 = (s32[]{:T(128)}, bf16[256,4,128]{2,0,1:T(8,128)(2,1)S(1)}, bf16[256,4,128]{2,0,1:T(8,128)(2,1)S(1)}, bf16[256,4,128]{2,0,1:T(8,128)(2,1)}, bf16[256...) while((s32[]{:T(128)}, ...), condition=%wide.region_26.27_spmd, body=%wide.region_25.26_spmd.sunk | while | flops 339403264 | bytes 13939170 | solution.py:182
  458.7 13.9 %collective-permute-done.6 = bf16[256,4,128]{2,0,1:T(8,128)(2,1)S(1)} collective-permute-done((bf16[256,4,128]{2,0,1:T(8,128)(2,1)S(1)}, bf16[256,4,128]{2,0,1:T(8,128)(2,1)S(1)}, u32[]{:S(2)}, u32[]{:S(2)}) %collective-permute-start.6) | collective-permute-done | bytes 262176 | tf_op jit(solution)/shard_map/while/body/eval_jaxpr/ppermute | solution.py:24
  484.7 14.1 %collective-permute-done.6 = bf16[256,4,128]{2,0,1:T(8,128)(2,1)S(1)} collective-permute-done((bf16[256,4,128]{2,0,1:T(8,128)(2,1)S(1)}, bf16[256,4,128]{2,0,1:T(8,128)(2,1)S(1)}, u32[]{:S(2)}, u32[]{:S(2)}) %collective-permute-start.6) | collective-permute-done | bytes 262176 | tf_op jit(solution)/shard_map/while/body/eval_jaxpr/ppermute | solution.py:24
  510.0 11.4 %collective-permute-done.6 = bf16[256,4,128]{2,0,1:T(8,128)(2,1)S(1)} collective-permute-done((bf16[256,4,128]{2,0,1:T(8,128)(2,1)S(1)}, bf16[256,4,128]{2,0,1:T(8,128)(2,1)S(1)}, u32[]{:S(2)}, u32[]{:S(2)}) %collective-permute-start.6) | collective-permute-done | bytes 262176 | tf_op jit(solution)/shard_map/while/body/eval_jaxpr/ppermute | solution.py:24
  534.8 134.4 %while.148 = (s32[]{:T(128)}, bf16[128,4,128]{2,0,1:T(8,128)(2,1)}, bf16[128,4,128]{2,0,1:T(8,128)(2,1)S(1)}, bf16[128,4,128]{2,0,1:T(8,128)(2,1)}, bf16[128,4,1...) while((s32[]{:T(128)}, bf16[128,4,128]{2,0,1:T(8,128)(2,1)}, ...), condition=%wide.region_31.32_spmd, body=%wide.region_30.31_spmd.sunk | while | flops 85094928 | bytes 5790178 | solution.py:182
  557.4 11.4 %collective-permute-done.10 = bf16[128,4,128]{2,0,1:T(8,128)(2,1)S(1)} collective-permute-done((bf16[128,4,128]{2,0,1:T(8,128)(2,1)}, bf16[128,4,128]{2,0,1:T(8,128)(2,1)S(1)}, u32[]{:S(2)}, u32[]{:S(2)}) %collective-permute-start.10) | collective-permute-done | bytes 131104 | tf_op jit(solution)/shard_map/while/body/eval_jaxpr/ppermute | solution.py:24
  578.2 11.5 %collective-permute-done.10 = bf16[128,4,128]{2,0,1:T(8,128)(2,1)S(1)} collective-permute-done((bf16[128,4,128]{2,0,1:T(8,128)(2,1)}, bf16[128,4,128]{2,0,1:T(8,128)(2,1)S(1)}, u32[]{:S(2)}, u32[]{:S(2)}) %collective-permute-start.10) | collective-permute-done | bytes 131104 | tf_op jit(solution)/shard_map/while/body/eval_jaxpr/ppermute | solution.py:24
  598.1 11.5 %collective-permute-done.10 = bf16[128,4,128]{2,0,1:T(8,128)(2,1)S(1)} collective-permute-done((bf16[128,4,128]{2,0,1:T(8,128)(2,1)}, bf16[128,4,128]{2,0,1:T(8,128)(2,1)S(1)}, u32[]{:S(2)}, u32[]{:S(2)}) %collective-permute-start.10) | collective-permute-done | bytes 131104 | tf_op jit(solution)/shard_map/while/body/eval_jaxpr/ppermute | solution.py:24
  617.1 11.5 %collective-permute-done.10 = bf16[128,4,128]{2,0,1:T(8,128)(2,1)S(1)} collective-permute-done((bf16[128,4,128]{2,0,1:T(8,128)(2,1)}, bf16[128,4,128]{2,0,1:T(8,128)(2,1)S(1)}, u32[]{:S(2)}, u32[]{:S(2)}) %collective-permute-start.10) | collective-permute-done | bytes 131104 | tf_op jit(solution)/shard_map/while/body/eval_jaxpr/ppermute | solution.py:24
  635.2 10.1 %collective-permute-done.10 = bf16[128,4,128]{2,0,1:T(8,128)(2,1)S(1)} collective-permute-done((bf16[128,4,128]{2,0,1:T(8,128)(2,1)}, bf16[128,4,128]{2,0,1:T(8,128)(2,1)S(1)}, u32[]{:S(2)}, u32[]{:S(2)}) %collective-permute-start.10) | collective-permute-done | bytes 131104 | tf_op jit(solution)/shard_map/while/body/eval_jaxpr/ppermute | solution.py:24
  651.2 10.1 %collective-permute-done.10 = bf16[128,4,128]{2,0,1:T(8,128)(2,1)S(1)} collective-permute-done((bf16[128,4,128]{2,0,1:T(8,128)(2,1)}, bf16[128,4,128]{2,0,1:T(8,128)(2,1)S(1)}, u32[]{:S(2)}, u32[]{:S(2)}) %collective-permute-start.10) | collective-permute-done | bytes 131104 | tf_op jit(solution)/shard_map/while/body/eval_jaxpr/ppermute | solution.py:24
  669.3 194.8 %while.149 = (s32[]{:T(128)}, bf16[64,4,128]{2,0,1:T(8,128)(2,1)S(1)}, bf16[64,4,128]{2,0,1:T(8,128)(2,1)S(1)}, bf16[64,4,128]{2,0,1:T(8,128)(2,1)S(1)}, bf16[64...) while((s32[]{:T(128)}, ...), condition=%wide.region_36.37_spmd, body=%wide.region_35.36_spmd.sunk | while | flops 21395728 | bytes 2600418 | solution.py:182
  669.8 10.0 %collective-permute-done.14 = bf16[64,4,128]{2,0,1:T(8,128)(2,1)S(1)} collective-permute-done((bf16[64,4,128]{2,0,1:T(8,128)(2,1)S(1)}, bf16[64,4,128]{2,0,1:T(8,128)(2,1)S(1)}, u32[]{:S(2)}, u32[]{:S(2)}) %collective-permute-start.14) | collective-permute-done | bytes 65568 | tf_op jit(solution)/shard_map/while/body/eval_jaxpr/ppermute | solution.py:24
  771.6 10.2 %collective-permute-done.14 = bf16[64,4,128]{2,0,1:T(8,128)(2,1)S(1)} collective-permute-done((bf16[64,4,128]{2,0,1:T(8,128)(2,1)S(1)}, bf16[64,4,128]{2,0,1:T(8,128)(2,1)S(1)}, u32[]{:S(2)}, u32[]{:S(2)}) %collective-permute-start.14) | collective-permute-done | bytes 65568 | tf_op jit(solution)/shard_map/while/body/eval_jaxpr/ppermute | solution.py:24
  786.8 10.3 %collective-permute-done.14 = bf16[64,4,128]{2,0,1:T(8,128)(2,1)S(1)} collective-permute-done((bf16[64,4,128]{2,0,1:T(8,128)(2,1)S(1)}, bf16[64,4,128]{2,0,1:T(8,128)(2,1)S(1)}, u32[]{:S(2)}, u32[]{:S(2)}) %collective-permute-start.14) | collective-permute-done | bytes 65568 | tf_op jit(solution)/shard_map/while/body/eval_jaxpr/ppermute | solution.py:24
  801.1 10.3 %collective-permute-done.14 = bf16[64,4,128]{2,0,1:T(8,128)(2,1)S(1)} collective-permute-done((bf16[64,4,128]{2,0,1:T(8,128)(2,1)S(1)}, bf16[64,4,128]{2,0,1:T(8,128)(2,1)S(1)}, u32[]{:S(2)}, u32[]{:S(2)}) %collective-permute-start.14) | collective-permute-done | bytes 65568 | tf_op jit(solution)/shard_map/while/body/eval_jaxpr/ppermute | solution.py:24
  (1186 shorter events, 658.6 us)
Async XLA Ops:
  7.2 35.5 %all-gather.2.cloned.1.call-start = ((), (), s32[]{:S(2)}) async-start(), calls=%async_computation | async-start | bytes 2621440 | tf_op jit(solution)/shard_map/all_gather | solution.py:210
  71.8 18.5 %collective-permute-start.1 = (bf16[256,4,128]{2,0,1:T(8,128)(2,1)}, bf16[256,4,128]{2,0,1:T(8,128)(2,1)S(1)}, u32[]{:S(2)}, u32[]{:S(2)}) collective-permute-start(bf16[256,4,128]{2,0,1:T(8,128)(2,1)} %get-tuple-element.3055), channel_id=1, source_target_pairs={{252,0},{0,4},{4,8},{8,12},{12,16},{16,20},{20,24},{24,28},{28,32}... | collective-permute-start | bytes 786440 | tf_op jit(solution)/shard_map/while/body/eval_jaxpr/ppermute | solution.py:24
  94.4 19.6 %collective-permute-start.1 = (bf16[256,4,128]{2,0,1:T(8,128)(2,1)}, bf16[256,4,128]{2,0,1:T(8,128)(2,1)S(1)}, u32[]{:S(2)}, u32[]{:S(2)}) collective-permute-start(bf16[256,4,128]{2,0,1:T(8,128)(2,1)} %get-tuple-element.3055), channel_id=1, source_target_pairs={{252,0},{0,4},{4,8},{8,12},{12,16},{16,20},{20,24},{24,28},{28,32}... | collective-permute-start | bytes 786440 | tf_op jit(solution)/shard_map/while/body/eval_jaxpr/ppermute | solution.py:24
  118.3 18.7 %collective-permute-start.1 = (bf16[256,4,128]{2,0,1:T(8,128)(2,1)}, bf16[256,4,128]{2,0,1:T(8,128)(2,1)S(1)}, u32[]{:S(2)}, u32[]{:S(2)}) collective-permute-start(bf16[256,4,128]{2,0,1:T(8,128)(2,1)} %get-tuple-element.3055), channel_id=1, source_target_pairs={{252,0},{0,4},{4,8},{8,12},{12,16},{16,20},{20,24},{24,28},{28,32}... | collective-permute-start | bytes 786440 | tf_op jit(solution)/shard_map/while/body/eval_jaxpr/ppermute | solution.py:24
  457.6 19.5 %collective-permute-start.7 = (bf16[256,4,128]{2,0,1:T(8,128)(2,1)S(1)}, bf16[256,4,128]{2,0,1:T(8,128)(2,1)S(1)}, u32[]{:S(2)}, u32[]{:S(2)}) collective-permute-start(bf16[256,4,128]{2,0,1:T(8,128)(2,1)S(1)} %get-tuple-element.3157), channel_id=1, source_target_pairs={{252,0},{0,4},{4,8},{8,12},{12,16},{16,20},{20,24},{24,28},{28,32}... | collective-permute-start | bytes 786440 | tf_op jit(solution)/shard_map/while/body/eval_jaxpr/ppermute | solution.py:24
  457.7 22.3 %collective-permute-start.8 = (bf16[256,4,128]{2,0,1:T(8,128)(2,1)}, bf16[256,4,128]{2,0,1:T(8,128)(2,1)S(1)}, u32[]{:S(2)}, u32[]{:S(2)}) collective-permute-start(bf16[256,4,128]{2,0,1:T(8,128)(2,1)} %get-tuple-element.3158), channel_id=1, source_target_pairs={{252,0},{0,4},{4,8},{8,12},{12,16},{16,20},{20,24},{24,28},{28,32}... | collective-permute-start | bytes 786440 | tf_op jit(solution)/shard_map/while/body/eval_jaxpr/ppermute | solution.py:24
  457.8 25.0 %collective-permute-start.9 = (bf16[256,4,128]{2,0,1:T(8,128)(2,1)}, bf16[256,4,128]{2,0,1:T(8,128)(2,1)S(1)}, u32[]{:S(2)}, u32[]{:S(2)}) collective-permute-start(bf16[256,4,128]{2,0,1:T(8,128)(2,1)} %get-tuple-element.3159), channel_id=1, source_target_pairs={{252,0},{0,4},{4,8},{8,12},{12,16},{16,20},{20,24},{24,28},{28,32}... | collective-permute-start | bytes 786440 | tf_op jit(solution)/shard_map/while/body/eval_jaxpr/ppermute | solution.py:24
  483.8 18.6 %collective-permute-start.7 = (bf16[256,4,128]{2,0,1:T(8,128)(2,1)S(1)}, bf16[256,4,128]{2,0,1:T(8,128)(2,1)S(1)}, u32[]{:S(2)}, u32[]{:S(2)}) collective-permute-start(bf16[256,4,128]{2,0,1:T(8,128)(2,1)S(1)} %get-tuple-element.3157), channel_id=1, source_target_pairs={{252,0},{0,4},{4,8},{8,12},{12,16},{16,20},{20,24},{24,28},{28,32}... | collective-permute-start | bytes 786440 | tf_op jit(solution)/shard_map/while/body/eval_jaxpr/ppermute | solution.py:24
  483.8 21.4 %collective-permute-start.8 = (bf16[256,4,128]{2,0,1:T(8,128)(2,1)}, bf16[256,4,128]{2,0,1:T(8,128)(2,1)S(1)}, u32[]{:S(2)}, u32[]{:S(2)}) collective-permute-start(bf16[256,4,128]{2,0,1:T(8,128)(2,1)} %get-tuple-element.3158), channel_id=1, source_target_pairs={{252,0},{0,4},{4,8},{8,12},{12,16},{16,20},{20,24},{24,28},{28,32}... | collective-permute-start | bytes 786440 | tf_op jit(solution)/shard_map/while/body/eval_jaxpr/ppermute | solution.py:24
  483.9 24.2 %collective-permute-start.9 = (bf16[256,4,128]{2,0,1:T(8,128)(2,1)}, bf16[256,4,128]{2,0,1:T(8,128)(2,1)S(1)}, u32[]{:S(2)}, u32[]{:S(2)}) collective-permute-start(bf16[256,4,128]{2,0,1:T(8,128)(2,1)} %get-tuple-element.3159), channel_id=1, source_target_pairs={{252,0},{0,4},{4,8},{8,12},{12,16},{16,20},{20,24},{24,28},{28,32}... | collective-permute-start | bytes 786440 | tf_op jit(solution)/shard_map/while/body/eval_jaxpr/ppermute | solution.py:24
  509.1 17.9 %collective-permute-start.8 = (bf16[256,4,128]{2,0,1:T(8,128)(2,1)}, bf16[256,4,128]{2,0,1:T(8,128)(2,1)S(1)}, u32[]{:S(2)}, u32[]{:S(2)}) collective-permute-start(bf16[256,4,128]{2,0,1:T(8,128)(2,1)} %get-tuple-element.3158), channel_id=1, source_target_pairs={{252,0},{0,4},{4,8},{8,12},{12,16},{16,20},{20,24},{24,28},{28,32}... | collective-permute-start | bytes 786440 | tf_op jit(solution)/shard_map/while/body/eval_jaxpr/ppermute | solution.py:24
  509.1 22.2 %collective-permute-start.9 = (bf16[256,4,128]{2,0,1:T(8,128)(2,1)}, bf16[256,4,128]{2,0,1:T(8,128)(2,1)S(1)}, u32[]{:S(2)}, u32[]{:S(2)}) collective-permute-start(bf16[256,4,128]{2,0,1:T(8,128)(2,1)} %get-tuple-element.3159), channel_id=1, source_target_pairs={{252,0},{0,4},{4,8},{8,12},{12,16},{16,20},{20,24},{24,28},{28,32}... | collective-permute-start | bytes 786440 | tf_op jit(solution)/shard_map/while/body/eval_jaxpr/ppermute | solution.py:24
  533.5 350.4 %collective-permute-start.18 = (bf16[256,4,128]{0,2,1:T(8,128)(2,1)S(1)}, bf16[256,4,128]{0,2,1:T(8,128)(2,1)}, u32[]{:S(2)}, u32[]{:S(2)}) collective-permute-start(bf16[256,4,128]{0,2,1:T(8,128)(2,1)S(1)} %copy.528), channel_id=1, source_target_pairs={{12,0},{16,4},{20,8},{24,12},{28,16},{32,20},{36,24},{40,28},{44,3... | collective-permute-start | bytes 786440 | tf_op jit(solution)/shard_map/ppermute | solution.py:24
  556.6 17.9 %collective-permute-start.12 = (bf16[128,4,128]{2,0,1:T(8,128)(2,1)}, bf16[128,4,128]{2,0,1:T(8,128)(2,1)S(1)}, u32[]{:S(2)}, u32[]{:S(2)}) collective-permute-start(bf16[128,4,128]{2,0,1:T(8,128)(2,1)} %get-tuple-element.3212), channel_id=1, source_target_pairs={{252,0},{0,4},{4,8},{8,12},{12,16},{16,20},{20,24},{24,28},{28,32}... | collective-permute-start | bytes 393224 | tf_op jit(solution)/shard_map/while/body/eval_jaxpr/ppermute | solution.py:24
  556.6 19.9 %collective-permute-start.13 = (bf16[128,4,128]{2,0,1:T(8,128)(2,1)}, bf16[128,4,128]{2,0,1:T(8,128)(2,1)S(1)}, u32[]{:S(2)}, u32[]{:S(2)}) collective-permute-start(bf16[128,4,128]{2,0,1:T(8,128)(2,1)} %get-tuple-element.3213), channel_id=1, source_target_pairs={{252,0},{0,4},{4,8},{8,12},{12,16},{16,20},{20,24},{24,28},{28,32}... | collective-permute-start | bytes 393224 | tf_op jit(solution)/shard_map/while/body/eval_jaxpr/ppermute | solution.py:24
  577.4 17.6 %collective-permute-start.12 = (bf16[128,4,128]{2,0,1:T(8,128)(2,1)}, bf16[128,4,128]{2,0,1:T(8,128)(2,1)S(1)}, u32[]{:S(2)}, u32[]{:S(2)}) collective-permute-start(bf16[128,4,128]{2,0,1:T(8,128)(2,1)} %get-tuple-element.3212), channel_id=1, source_target_pairs={{252,0},{0,4},{4,8},{8,12},{12,16},{16,20},{20,24},{24,28},{28,32}... | collective-permute-start | bytes 393224 | tf_op jit(solution)/shard_map/while/body/eval_jaxpr/ppermute | solution.py:24
  577.4 19.0 %collective-permute-start.13 = (bf16[128,4,128]{2,0,1:T(8,128)(2,1)}, bf16[128,4,128]{2,0,1:T(8,128)(2,1)S(1)}, u32[]{:S(2)}, u32[]{:S(2)}) collective-permute-start(bf16[128,4,128]{2,0,1:T(8,128)(2,1)} %get-tuple-element.3213), channel_id=1, source_target_pairs={{252,0},{0,4},{4,8},{8,12},{12,16},{16,20},{20,24},{24,28},{28,32}... | collective-permute-start | bytes 393224 | tf_op jit(solution)/shard_map/while/body/eval_jaxpr/ppermute | solution.py:24
  597.3 16.7 %collective-permute-start.12 = (bf16[128,4,128]{2,0,1:T(8,128)(2,1)}, bf16[128,4,128]{2,0,1:T(8,128)(2,1)S(1)}, u32[]{:S(2)}, u32[]{:S(2)}) collective-permute-start(bf16[128,4,128]{2,0,1:T(8,128)(2,1)} %get-tuple-element.3212), channel_id=1, source_target_pairs={{252,0},{0,4},{4,8},{8,12},{12,16},{16,20},{20,24},{24,28},{28,32}... | collective-permute-start | bytes 393224 | tf_op jit(solution)/shard_map/while/body/eval_jaxpr/ppermute | solution.py:24
  597.3 18.1 %collective-permute-start.13 = (bf16[128,4,128]{2,0,1:T(8,128)(2,1)}, bf16[128,4,128]{2,0,1:T(8,128)(2,1)S(1)}, u32[]{:S(2)}, u32[]{:S(2)}) collective-permute-start(bf16[128,4,128]{2,0,1:T(8,128)(2,1)} %get-tuple-element.3213), channel_id=1, source_target_pairs={{252,0},{0,4},{4,8},{8,12},{12,16},{16,20},{20,24},{24,28},{28,32}... | collective-permute-start | bytes 393224 | tf_op jit(solution)/shard_map/while/body/eval_jaxpr/ppermute | solution.py:24
  616.3 17.2 %collective-permute-start.13 = (bf16[128,4,128]{2,0,1:T(8,128)(2,1)}, bf16[128,4,128]{2,0,1:T(8,128)(2,1)S(1)}, u32[]{:S(2)}, u32[]{:S(2)}) collective-permute-start(bf16[128,4,128]{2,0,1:T(8,128)(2,1)} %get-tuple-element.3213), channel_id=1, source_target_pairs={{252,0},{0,4},{4,8},{8,12},{12,16},{16,20},{20,24},{24,28},{28,32}... | collective-permute-start | bytes 393224 | tf_op jit(solution)/shard_map/while/body/eval_jaxpr/ppermute | solution.py:24
  650.4 17.9 %collective-permute-start.13 = (bf16[128,4,128]{2,0,1:T(8,128)(2,1)}, bf16[128,4,128]{2,0,1:T(8,128)(2,1)S(1)}, u32[]{:S(2)}, u32[]{:S(2)}) collective-permute-start(bf16[128,4,128]{2,0,1:T(8,128)(2,1)} %get-tuple-element.3213), channel_id=1, source_target_pairs={{252,0},{0,4},{4,8},{8,12},{12,16},{16,20},{20,24},{24,28},{28,32}... | collective-permute-start | bytes 393224 | tf_op jit(solution)/shard_map/while/body/eval_jaxpr/ppermute | solution.py:24
  864.1 19.9 %collective-permute-start.21 = (bf16[256,4,128]{0,2,1:T(8,128)(2,1)S(1)}, bf16[256,4,128]{0,2,1:T(8,128)(2,1)}, u32[]{:S(2)}, u32[]{:S(2)}) collective-permute-start(bf16[256,4,128]{0,2,1:T(8,128)(2,1)S(1)} %copy.534), channel_id=1, source_target_pairs={{12,0},{16,4},{20,8},{24,12},{28,16},{32,20},{36,24},{40,28},{44,3... | collective-permute-start | bytes 786440 | tf_op jit(solution)/shard_map/ppermute | solution.py:24
  867.0 16.7 %collective-permute-start.22 = (bf16[128,4,128]{2,0,1:T(8,128)(2,1)S(1)}, bf16[128,4,128]{2,0,1:T(8,128)(2,1)S(1)}, u32[]{:S(2)}, u32[]{:S(2)}) collective-permute-start(bf16[128,4,128]{2,0,1:T(8,128)(2,1)S(1)} %copy-done.37), channel_id=1, source_target_pairs={{28,0},{32,4},{36,8},{40,12},{44,16},{48,20},{52,24},{56,28},{60,3... | collective-permute-start | bytes 393224 | tf_op jit(solution)/shard_map/ppermute | solution.py:24
  867.0 16.8 %collective-permute-start.19 = (bf16[128,4,128]{2,0,1:T(8,128)(2,1)S(1)}, bf16[128,4,128]{2,0,1:T(8,128)(2,1)S(1)}, u32[]{:S(2)}, u32[]{:S(2)}) collective-permute-start(bf16[128,4,128]{2,0,1:T(8,128)(2,1)S(1)} %copy-done.36), channel_id=1, source_target_pairs={{28,0},{32,4},{36,8},{40,12},{44,16},{48,20},{52,24},{56,28},{60,3... | collective-permute-start | bytes 393224 | tf_op jit(solution)/shard_map/ppermute | solution.py:24
  (221 other events, 6900.4 us)
Sparse Core Ops, SparseCore 0:
  9.8 32.8 all-gather.1
where the time goes:
time: 902 us; the launch traced here: 898 us
  waiting for transfers between devices  624 us (69%)
  matrix products  112 us (12%)
  local copies, waits for them, and re-layouts  60.7 us (7%)
  other arithmetic  57.5 us (6%)
  starting transfers between devices  22.4 us (2%)
  between operations  15.9 us (2%)
    ppermute x156, waiting for transfers between devices, passed_along(): return lax.ppermute(block, axis, route)  601 us
    select_n x53, other arithmetic, linked_pairs(): return (query_pos // segment == key_pos // segment) & (key_pos <= query_pos)  25.9 us
    ppermute x156, starting transfers between devices, passed_along(): return lax.ppermute(block, axis, route)  22.3 us
    all_gather x1, waiting for transfers between devices, local(): lax.all_gather(out_grad, 'tp', axis=1, tiled=True)  21.8 us
  transfers between devices with their start and end apart: 157, of which 144 were waited for; matrix products, arithmetic and copies ran while one was open for 13% of the time, Pallas kernels for 0%

commit v1 on v0

--- a/solution.py
+++ b/solution.py
@@ -207,7 +207,9 @@
     value_rows = values.reshape(tok_rows, head_count, head_width)
     grad_out = jnp.einsum(
         "td,fd->tf",
-        lax.all_gather(out_grad, "tp", axis=1, tiled=True),
+        jnp.concatenate(
+            lax.all_to_all(jnp.stack([out_grad] * lax.axis_size("tp")), "tp", 0, 0), axis=1
+        ),
         w_out,
         preferred_element_type=jnp.float32,
     )

time: 902 us -> 893 us (0.990)
  between operations: 15.9 us -> 2.89 us
  loops' own time: 5.49 us -> 16.5 us
    all_gather x1 -> x0, waiting for transfers between devices: 21.8 us -> none  [local(): lax.all_gather(out_grad, 'tp', axis=1, tiled=True)]
    all_to_all x0 -> x1, waiting for transfers between devices: none -> 15.7 us  [local(): lax.all_to_all(jnp.stack([out_grad] * lax.axis_size('tp')), 'tp', 0, 0)]
    another operation x3, loops' own time: 2.6 us -> 13.6 us  [forward_relay(): lax.fori_loop(1, relay_turns + 1, forward_turn_body, (key_pair, running,...]
    ppermute x156, waiting for transfers between devices: 601 us -> 611 us  [passed_along(): return lax.ppermute(block, axis, route)]
  transfers between devices with their start and end apart: 157 -> 157, of which waited for: 144 -> 144; matrix products, arithmetic and copies ran while one was open for 13% -> 12% of each run, Pallas kernels for 0% -> 0%
where the time goes in v1:
time: 893 us; the launch traced here: 884 us
  waiting for transfers between devices  626 us (70%)
  matrix products  109 us (12%)
  local copies, waits for them, and re-layouts  52.4 us (6%)
  other arithmetic  49 us (5%)
  starting transfers between devices  27.4 us (3%)
  loops' own time  16.5 us (2%)
    ppermute x156, waiting for transfers between devices, passed_along(): return lax.ppermute(block, axis, route)  611 us
    ppermute x156, starting transfers between devices, passed_along(): return lax.ppermute(block, axis, route)  20.7 us
    dot_general x28, matrix products, forward_tile(): jnp.einsum('hab,bhd->ahd', weights_high, key_pair[1], preferred_element_t...  18.2 us
  transfers between devices with their start and end apart: 157, of which 144 were waited for; matrix products, arithmetic and copies ran while one was open for 12% of the time, Pallas kernels for 0%

profile of v1, /device:TPU:8, one launch (start us, length us, event | category | flops | bytes accessed | tf_op | source)
XLA Modules:
  0.0 883.6 jit_solution(608756024212365701)
XLA Ops:
  18.5 15.7 %all-to-all-done = bf16[4,256,1024]{1,2,0:T(8,128)(2,1)} async-done(((bf16[4,256,1024]{1,2,0:T(8,128)(2,1)}), bf16[4,256,1024]{1,2,0:T(8,128)(2,1)}, u32[]{:S(2)}, u32[]{:S(2)}) %all-to-all-start) | async-done | bytes 2097184 | tf_op jit(solution)/shard_map/all_to_all | solution.py:211
  60.9 70.5 %while.144 = (s32[]{:T(128)}, bf16[256,4,128]{2,0,1:T(8,128)(2,1)}, bf16[256,4,128]{2,0,1:T(8,128)(2,1)}, f32[256,4]{0,1:T(4,128)S(1)}, f32[256,4]{0,1:T(4,128)S...) while((s32[]{:T(128)}, bf16[256,4,128]{2,0,1:T(8,128)(2,1)}, ...), condition=%wide.region_5.6_spmd, body=%wide.region_2.5_spmd.sunk | while | flops 208857616 | bytes 10641786 | solution.py:121
  63.8 12.9 %collective-permute-done = bf16[256,4,128]{2,0,1:T(8,128)(2,1)S(1)} collective-permute-done((bf16[256,4,128]{2,0,1:T(8,128)(2,1)}, bf16[256,4,128]{2,0,1:T(8,128)(2,1)S(1)}, u32[]{:S(2)}, u32[]{:S(2)}) %collective-permute-start) | collective-permute-done | bytes 262176 | tf_op jit(solution)/shard_map/while/body/eval_jaxpr/ppermute | solution.py:24
  86.6 14.3 %collective-permute-done = bf16[256,4,128]{2,0,1:T(8,128)(2,1)S(1)} collective-permute-done((bf16[256,4,128]{2,0,1:T(8,128)(2,1)}, bf16[256,4,128]{2,0,1:T(8,128)(2,1)S(1)}, u32[]{:S(2)}, u32[]{:S(2)}) %collective-permute-start) | collective-permute-done | bytes 262176 | tf_op jit(solution)/shard_map/while/body/eval_jaxpr/ppermute | solution.py:24
  110.0 14.3 %collective-permute-done = bf16[256,4,128]{2,0,1:T(8,128)(2,1)S(1)} collective-permute-done((bf16[256,4,128]{2,0,1:T(8,128)(2,1)}, bf16[256,4,128]{2,0,1:T(8,128)(2,1)S(1)}, u32[]{:S(2)}, u32[]{:S(2)}) %collective-permute-start) | collective-permute-done | bytes 262176 | tf_op jit(solution)/shard_map/while/body/eval_jaxpr/ppermute | solution.py:24
  132.1 185.1 %while.146 = (s32[]{:T(128)}, bf16[64,4,128]{2,0,1:T(8,128)(2,1)S(1)}, bf16[64,4,128]{2,0,1:T(8,128)(2,1)S(1)}, f32[64,4]{0,1:T(4,128)S(1)}, f32[64,4]{0,1:T(4,1...) while((s32[]{:T(128)}, ...), condition=%wide.region_23.24_spmd, body=%wide.region_20.23_spmd.sunk | while | flops 13138703 | bytes 1874298 | solution.py:121
  212.7 10.5 %collective-permute-done.4 = bf16[64,4,128]{2,0,1:T(8,128)(2,1)S(1)} collective-permute-done((bf16[64,4,128]{2,0,1:T(8,128)(2,1)S(1)}, bf16[64,4,128]{2,0,1:T(8,128)(2,1)S(1)}, u32[]{:S(2)}, u32[]{:S(2)}) %collective-permute-start.4) | collective-permute-done | bytes 65568 | tf_op jit(solution)/shard_map/while/body/eval_jaxpr/ppermute | solution.py:24
  225.5 10.3 %collective-permute-done.4 = bf16[64,4,128]{2,0,1:T(8,128)(2,1)S(1)} collective-permute-done((bf16[64,4,128]{2,0,1:T(8,128)(2,1)S(1)}, bf16[64,4,128]{2,0,1:T(8,128)(2,1)S(1)}, u32[]{:S(2)}, u32[]{:S(2)}) %collective-permute-start.4) | collective-permute-done | bytes 65568 | tf_op jit(solution)/shard_map/while/body/eval_jaxpr/ppermute | solution.py:24
  320.3 99.2 %while.145 = (s32[]{:T(128)}, bf16[128,4,128]{2,0,1:T(8,128)(2,1)S(1)}, bf16[128,4,128]{2,0,1:T(8,128)(2,1)S(1)}, f32[128,4]{0,1:T(4,128)S(1)}, f32[128,4]{0,1:T...) while((s32[]{:T(128)}, ...), condition=%wide.region_14.15_spmd, body=%wide.region_11.14_spmd.sunk | while | flops 52327952 | bytes 4272506 | solution.py:121
  451.1 74.7 %while.147 = (s32[]{:T(128)}, bf16[256,4,128]{2,0,1:T(8,128)(2,1)S(1)}, bf16[256,4,128]{2,0,1:T(8,128)(2,1)S(1)}, bf16[256,4,128]{2,0,1:T(8,128)(2,1)}, bf16[256...) while((s32[]{:T(128)}, ...), condition=%wide.region_26.27_spmd, body=%wide.region_25.26_spmd.sunk | while | flops 339403264 | bytes 13939170 | solution.py:182
  452.2 13.9 %collective-permute-done.6 = bf16[256,4,128]{2,0,1:T(8,128)(2,1)S(1)} collective-permute-done((bf16[256,4,128]{2,0,1:T(8,128)(2,1)S(1)}, bf16[256,4,128]{2,0,1:T(8,128)(2,1)S(1)}, u32[]{:S(2)}, u32[]{:S(2)}) %collective-permute-start.6) | collective-permute-done | bytes 262176 | tf_op jit(solution)/shard_map/while/body/eval_jaxpr/ppermute | solution.py:24
  478.2 14.1 %collective-permute-done.6 = bf16[256,4,128]{2,0,1:T(8,128)(2,1)S(1)} collective-permute-done((bf16[256,4,128]{2,0,1:T(8,128)(2,1)S(1)}, bf16[256,4,128]{2,0,1:T(8,128)(2,1)S(1)}, u32[]{:S(2)}, u32[]{:S(2)}) %collective-permute-start.6) | collective-permute-done | bytes 262176 | tf_op jit(solution)/shard_map/while/body/eval_jaxpr/ppermute | solution.py:24
  503.4 11.5 %collective-permute-done.6 = bf16[256,4,128]{2,0,1:T(8,128)(2,1)S(1)} collective-permute-done((bf16[256,4,128]{2,0,1:T(8,128)(2,1)S(1)}, bf16[256,4,128]{2,0,1:T(8,128)(2,1)S(1)}, u32[]{:S(2)}, u32[]{:S(2)}) %collective-permute-start.6) | collective-permute-done | bytes 262176 | tf_op jit(solution)/shard_map/while/body/eval_jaxpr/ppermute | solution.py:24
  528.1 134.4 %while.148 = (s32[]{:T(128)}, bf16[128,4,128]{2,0,1:T(8,128)(2,1)}, bf16[128,4,128]{2,0,1:T(8,128)(2,1)S(1)}, bf16[128,4,128]{2,0,1:T(8,128)(2,1)}, bf16[128,4,1...) while((s32[]{:T(128)}, bf16[128,4,128]{2,0,1:T(8,128)(2,1)}, ...), condition=%wide.region_31.32_spmd, body=%wide.region_30.31_spmd.sunk | while | flops 85094928 | bytes 5790178 | solution.py:182
  550.6 11.4 %collective-permute-done.10 = bf16[128,4,128]{2,0,1:T(8,128)(2,1)S(1)} collective-permute-done((bf16[128,4,128]{2,0,1:T(8,128)(2,1)}, bf16[128,4,128]{2,0,1:T(8,128)(2,1)S(1)}, u32[]{:S(2)}, u32[]{:S(2)}) %collective-permute-start.10) | collective-permute-done | bytes 131104 | tf_op jit(solution)/shard_map/while/body/eval_jaxpr/ppermute | solution.py:24
  571.4 11.5 %collective-permute-done.10 = bf16[128,4,128]{2,0,1:T(8,128)(2,1)S(1)} collective-permute-done((bf16[128,4,128]{2,0,1:T(8,128)(2,1)}, bf16[128,4,128]{2,0,1:T(8,128)(2,1)S(1)}, u32[]{:S(2)}, u32[]{:S(2)}) %collective-permute-start.10) | collective-permute-done | bytes 131104 | tf_op jit(solution)/shard_map/while/body/eval_jaxpr/ppermute | solution.py:24
  591.4 11.5 %collective-permute-done.10 = bf16[128,4,128]{2,0,1:T(8,128)(2,1)S(1)} collective-permute-done((bf16[128,4,128]{2,0,1:T(8,128)(2,1)}, bf16[128,4,128]{2,0,1:T(8,128)(2,1)S(1)}, u32[]{:S(2)}, u32[]{:S(2)}) %collective-permute-start.10) | collective-permute-done | bytes 131104 | tf_op jit(solution)/shard_map/while/body/eval_jaxpr/ppermute | solution.py:24
  610.4 11.5 %collective-permute-done.10 = bf16[128,4,128]{2,0,1:T(8,128)(2,1)S(1)} collective-permute-done((bf16[128,4,128]{2,0,1:T(8,128)(2,1)}, bf16[128,4,128]{2,0,1:T(8,128)(2,1)S(1)}, u32[]{:S(2)}, u32[]{:S(2)}) %collective-permute-start.10) | collective-permute-done | bytes 131104 | tf_op jit(solution)/shard_map/while/body/eval_jaxpr/ppermute | solution.py:24
  628.5 10.1 %collective-permute-done.10 = bf16[128,4,128]{2,0,1:T(8,128)(2,1)S(1)} collective-permute-done((bf16[128,4,128]{2,0,1:T(8,128)(2,1)}, bf16[128,4,128]{2,0,1:T(8,128)(2,1)S(1)}, u32[]{:S(2)}, u32[]{:S(2)}) %collective-permute-start.10) | collective-permute-done | bytes 131104 | tf_op jit(solution)/shard_map/while/body/eval_jaxpr/ppermute | solution.py:24
  644.5 10.1 %collective-permute-done.10 = bf16[128,4,128]{2,0,1:T(8,128)(2,1)S(1)} collective-permute-done((bf16[128,4,128]{2,0,1:T(8,128)(2,1)}, bf16[128,4,128]{2,0,1:T(8,128)(2,1)S(1)}, u32[]{:S(2)}, u32[]{:S(2)}) %collective-permute-start.10) | collective-permute-done | bytes 131104 | tf_op jit(solution)/shard_map/while/body/eval_jaxpr/ppermute | solution.py:24
  662.6 194.8 %while.149 = (s32[]{:T(128)}, bf16[64,4,128]{2,0,1:T(8,128)(2,1)S(1)}, bf16[64,4,128]{2,0,1:T(8,128)(2,1)S(1)}, bf16[64,4,128]{2,0,1:T(8,128)(2,1)S(1)}, bf16[64...) while((s32[]{:T(128)}, ...), condition=%wide.region_36.37_spmd, body=%wide.region_35.36_spmd.sunk | while | flops 21395728 | bytes 2600418 | solution.py:182
  764.9 10.3 %collective-permute-done.14 = bf16[64,4,128]{2,0,1:T(8,128)(2,1)S(1)} collective-permute-done((bf16[64,4,128]{2,0,1:T(8,128)(2,1)S(1)}, bf16[64,4,128]{2,0,1:T(8,128)(2,1)S(1)}, u32[]{:S(2)}, u32[]{:S(2)}) %collective-permute-start.14) | collective-permute-done | bytes 65568 | tf_op jit(solution)/shard_map/while/body/eval_jaxpr/ppermute | solution.py:24
  780.1 10.3 %collective-permute-done.14 = bf16[64,4,128]{2,0,1:T(8,128)(2,1)S(1)} collective-permute-done((bf16[64,4,128]{2,0,1:T(8,128)(2,1)S(1)}, bf16[64,4,128]{2,0,1:T(8,128)(2,1)S(1)}, u32[]{:S(2)}, u32[]{:S(2)}) %collective-permute-start.14) | collective-permute-done | bytes 65568 | tf_op jit(solution)/shard_map/while/body/eval_jaxpr/ppermute | solution.py:24
  794.5 10.3 %collective-permute-done.14 = bf16[64,4,128]{2,0,1:T(8,128)(2,1)S(1)} collective-permute-done((bf16[64,4,128]{2,0,1:T(8,128)(2,1)S(1)}, bf16[64,4,128]{2,0,1:T(8,128)(2,1)S(1)}, u32[]{:S(2)}, u32[]{:S(2)}) %collective-permute-start.14) | collective-permute-done | bytes 65568 | tf_op jit(solution)/shard_map/while/body/eval_jaxpr/ppermute | solution.py:24
  (1225 shorter events, 649.8 us)
Async XLA Ops:
  3.4 30.9 %all-to-all-start = ((bf16[4,256,1024]{1,2,0:T(8,128)(2,1)}), bf16[4,256,1024]{1,2,0:T(8,128)(2,1)}, u32[]{:S(2)}, u32[]{:S(2)}) async-start(bf16[4,256,1024]{1,2,0:T(8,128)(2,1)} %stack.2), calls=%async_computation | async-start | bytes 4194304 | tf_op jit(solution)/shard_map/all_to_all | solution.py:211
  61.2 20.4 %collective-permute-start.1 = (bf16[256,4,128]{2,0,1:T(8,128)(2,1)}, bf16[256,4,128]{2,0,1:T(8,128)(2,1)S(1)}, u32[]{:S(2)}, u32[]{:S(2)}) collective-permute-start(bf16[256,4,128]{2,0,1:T(8,128)(2,1)} %get-tuple-element.3055), channel_id=1, source_target_pairs={{252,0},{0,4},{4,8},{8,12},{12,16},{16,20},{20,24},{24,28},{28,32}... | collective-permute-start | bytes 786440 | tf_op jit(solution)/shard_map/while/body/eval_jaxpr/ppermute | solution.py:24
  85.8 19.1 %collective-permute-start.1 = (bf16[256,4,128]{2,0,1:T(8,128)(2,1)}, bf16[256,4,128]{2,0,1:T(8,128)(2,1)S(1)}, u32[]{:S(2)}, u32[]{:S(2)}) collective-permute-start(bf16[256,4,128]{2,0,1:T(8,128)(2,1)} %get-tuple-element.3055), channel_id=1, source_target_pairs={{252,0},{0,4},{4,8},{8,12},{12,16},{16,20},{20,24},{24,28},{28,32}... | collective-permute-start | bytes 786440 | tf_op jit(solution)/shard_map/while/body/eval_jaxpr/ppermute | solution.py:24
  109.1 18.2 %collective-permute-start.1 = (bf16[256,4,128]{2,0,1:T(8,128)(2,1)}, bf16[256,4,128]{2,0,1:T(8,128)(2,1)S(1)}, u32[]{:S(2)}, u32[]{:S(2)}) collective-permute-start(bf16[256,4,128]{2,0,1:T(8,128)(2,1)} %get-tuple-element.3055), channel_id=1, source_target_pairs={{252,0},{0,4},{4,8},{8,12},{12,16},{16,20},{20,24},{24,28},{28,32}... | collective-permute-start | bytes 786440 | tf_op jit(solution)/shard_map/while/body/eval_jaxpr/ppermute | solution.py:24
  451.2 19.5 %collective-permute-start.7 = (bf16[256,4,128]{2,0,1:T(8,128)(2,1)S(1)}, bf16[256,4,128]{2,0,1:T(8,128)(2,1)S(1)}, u32[]{:S(2)}, u32[]{:S(2)}) collective-permute-start(bf16[256,4,128]{2,0,1:T(8,128)(2,1)S(1)} %get-tuple-element.3157), channel_id=1, source_target_pairs={{252,0},{0,4},{4,8},{8,12},{12,16},{16,20},{20,24},{24,28},{28,32}... | collective-permute-start | bytes 786440 | tf_op jit(solution)/shard_map/while/body/eval_jaxpr/ppermute | solution.py:24
  451.3 22.2 %collective-permute-start.8 = (bf16[256,4,128]{2,0,1:T(8,128)(2,1)}, bf16[256,4,128]{2,0,1:T(8,128)(2,1)S(1)}, u32[]{:S(2)}, u32[]{:S(2)}) collective-permute-start(bf16[256,4,128]{2,0,1:T(8,128)(2,1)} %get-tuple-element.3158), channel_id=1, source_target_pairs={{252,0},{0,4},{4,8},{8,12},{12,16},{16,20},{20,24},{24,28},{28,32}... | collective-permute-start | bytes 786440 | tf_op jit(solution)/shard_map/while/body/eval_jaxpr/ppermute | solution.py:24
  451.4 24.9 %collective-permute-start.9 = (bf16[256,4,128]{2,0,1:T(8,128)(2,1)}, bf16[256,4,128]{2,0,1:T(8,128)(2,1)S(1)}, u32[]{:S(2)}, u32[]{:S(2)}) collective-permute-start(bf16[256,4,128]{2,0,1:T(8,128)(2,1)} %get-tuple-element.3159), channel_id=1, source_target_pairs={{252,0},{0,4},{4,8},{8,12},{12,16},{16,20},{20,24},{24,28},{28,32}... | collective-permute-start | bytes 786440 | tf_op jit(solution)/shard_map/while/body/eval_jaxpr/ppermute | solution.py:24
  477.3 18.5 %collective-permute-start.7 = (bf16[256,4,128]{2,0,1:T(8,128)(2,1)S(1)}, bf16[256,4,128]{2,0,1:T(8,128)(2,1)S(1)}, u32[]{:S(2)}, u32[]{:S(2)}) collective-permute-start(bf16[256,4,128]{2,0,1:T(8,128)(2,1)S(1)} %get-tuple-element.3157), channel_id=1, source_target_pairs={{252,0},{0,4},{4,8},{8,12},{12,16},{16,20},{20,24},{24,28},{28,32}... | collective-permute-start | bytes 786440 | tf_op jit(solution)/shard_map/while/body/eval_jaxpr/ppermute | solution.py:24
  477.3 21.3 %collective-permute-start.8 = (bf16[256,4,128]{2,0,1:T(8,128)(2,1)}, bf16[256,4,128]{2,0,1:T(8,128)(2,1)S(1)}, u32[]{:S(2)}, u32[]{:S(2)}) collective-permute-start(bf16[256,4,128]{2,0,1:T(8,128)(2,1)} %get-tuple-element.3158), channel_id=1, source_target_pairs={{252,0},{0,4},{4,8},{8,12},{12,16},{16,20},{20,24},{24,28},{28,32}... | collective-permute-start | bytes 786440 | tf_op jit(solution)/shard_map/while/body/eval_jaxpr/ppermute | solution.py:24
  477.3 24.1 %collective-permute-start.9 = (bf16[256,4,128]{2,0,1:T(8,128)(2,1)}, bf16[256,4,128]{2,0,1:T(8,128)(2,1)S(1)}, u32[]{:S(2)}, u32[]{:S(2)}) collective-permute-start(bf16[256,4,128]{2,0,1:T(8,128)(2,1)} %get-tuple-element.3159), channel_id=1, source_target_pairs={{252,0},{0,4},{4,8},{8,12},{12,16},{16,20},{20,24},{24,28},{28,32}... | collective-permute-start | bytes 786440 | tf_op jit(solution)/shard_map/while/body/eval_jaxpr/ppermute | solution.py:24
  502.5 17.9 %collective-permute-start.8 = (bf16[256,4,128]{2,0,1:T(8,128)(2,1)}, bf16[256,4,128]{2,0,1:T(8,128)(2,1)S(1)}, u32[]{:S(2)}, u32[]{:S(2)}) collective-permute-start(bf16[256,4,128]{2,0,1:T(8,128)(2,1)} %get-tuple-element.3158), channel_id=1, source_target_pairs={{252,0},{0,4},{4,8},{8,12},{12,16},{16,20},{20,24},{24,28},{28,32}... | collective-permute-start | bytes 786440 | tf_op jit(solution)/shard_map/while/body/eval_jaxpr/ppermute | solution.py:24
  502.5 22.2 %collective-permute-start.9 = (bf16[256,4,128]{2,0,1:T(8,128)(2,1)}, bf16[256,4,128]{2,0,1:T(8,128)(2,1)S(1)}, u32[]{:S(2)}, u32[]{:S(2)}) collective-permute-start(bf16[256,4,128]{2,0,1:T(8,128)(2,1)} %get-tuple-element.3159), channel_id=1, source_target_pairs={{252,0},{0,4},{4,8},{8,12},{12,16},{16,20},{20,24},{24,28},{28,32}... | collective-permute-start | bytes 786440 | tf_op jit(solution)/shard_map/while/body/eval_jaxpr/ppermute | solution.py:24
  526.9 350.4 %collective-permute-start.18 = (bf16[256,4,128]{0,2,1:T(8,128)(2,1)S(1)}, bf16[256,4,128]{0,2,1:T(8,128)(2,1)S(1)}, u32[]{:S(2)}, u32[]{:S(2)}) collective-permute-start(bf16[256,4,128]{0,2,1:T(8,128)(2,1)S(1)} %copy.532), channel_id=1, source_target_pairs={{12,0},{16,4},{20,8},{24,12},{28,16},{32,20},{36,24},{40,28},{44,3... | collective-permute-start | bytes 786440 | tf_op jit(solution)/shard_map/ppermute | solution.py:24
  549.8 17.9 %collective-permute-start.12 = (bf16[128,4,128]{2,0,1:T(8,128)(2,1)}, bf16[128,4,128]{2,0,1:T(8,128)(2,1)S(1)}, u32[]{:S(2)}, u32[]{:S(2)}) collective-permute-start(bf16[128,4,128]{2,0,1:T(8,128)(2,1)} %get-tuple-element.3212), channel_id=1, source_target_pairs={{252,0},{0,4},{4,8},{8,12},{12,16},{16,20},{20,24},{24,28},{28,32}... | collective-permute-start | bytes 393224 | tf_op jit(solution)/shard_map/while/body/eval_jaxpr/ppermute | solution.py:24
  549.8 19.9 %collective-permute-start.13 = (bf16[128,4,128]{2,0,1:T(8,128)(2,1)}, bf16[128,4,128]{2,0,1:T(8,128)(2,1)S(1)}, u32[]{:S(2)}, u32[]{:S(2)}) collective-permute-start(bf16[128,4,128]{2,0,1:T(8,128)(2,1)} %get-tuple-element.3213), channel_id=1, source_target_pairs={{252,0},{0,4},{4,8},{8,12},{12,16},{16,20},{20,24},{24,28},{28,32}... | collective-permute-start | bytes 393224 | tf_op jit(solution)/shard_map/while/body/eval_jaxpr/ppermute | solution.py:24
  570.6 17.6 %collective-permute-start.12 = (bf16[128,4,128]{2,0,1:T(8,128)(2,1)}, bf16[128,4,128]{2,0,1:T(8,128)(2,1)S(1)}, u32[]{:S(2)}, u32[]{:S(2)}) collective-permute-start(bf16[128,4,128]{2,0,1:T(8,128)(2,1)} %get-tuple-element.3212), channel_id=1, source_target_pairs={{252,0},{0,4},{4,8},{8,12},{12,16},{16,20},{20,24},{24,28},{28,32}... | collective-permute-start | bytes 393224 | tf_op jit(solution)/shard_map/while/body/eval_jaxpr/ppermute | solution.py:24
  570.6 19.0 %collective-permute-start.13 = (bf16[128,4,128]{2,0,1:T(8,128)(2,1)}, bf16[128,4,128]{2,0,1:T(8,128)(2,1)S(1)}, u32[]{:S(2)}, u32[]{:S(2)}) collective-permute-start(bf16[128,4,128]{2,0,1:T(8,128)(2,1)} %get-tuple-element.3213), channel_id=1, source_target_pairs={{252,0},{0,4},{4,8},{8,12},{12,16},{16,20},{20,24},{24,28},{28,32}... | collective-permute-start | bytes 393224 | tf_op jit(solution)/shard_map/while/body/eval_jaxpr/ppermute | solution.py:24
  590.5 16.7 %collective-permute-start.12 = (bf16[128,4,128]{2,0,1:T(8,128)(2,1)}, bf16[128,4,128]{2,0,1:T(8,128)(2,1)S(1)}, u32[]{:S(2)}, u32[]{:S(2)}) collective-permute-start(bf16[128,4,128]{2,0,1:T(8,128)(2,1)} %get-tuple-element.3212), channel_id=1, source_target_pairs={{252,0},{0,4},{4,8},{8,12},{12,16},{16,20},{20,24},{24,28},{28,32}... | collective-permute-start | bytes 393224 | tf_op jit(solution)/shard_map/while/body/eval_jaxpr/ppermute | solution.py:24
  590.6 18.1 %collective-permute-start.13 = (bf16[128,4,128]{2,0,1:T(8,128)(2,1)}, bf16[128,4,128]{2,0,1:T(8,128)(2,1)S(1)}, u32[]{:S(2)}, u32[]{:S(2)}) collective-permute-start(bf16[128,4,128]{2,0,1:T(8,128)(2,1)} %get-tuple-element.3213), channel_id=1, source_target_pairs={{252,0},{0,4},{4,8},{8,12},{12,16},{16,20},{20,24},{24,28},{28,32}... | collective-permute-start | bytes 393224 | tf_op jit(solution)/shard_map/while/body/eval_jaxpr/ppermute | solution.py:24
  609.6 17.2 %collective-permute-start.13 = (bf16[128,4,128]{2,0,1:T(8,128)(2,1)}, bf16[128,4,128]{2,0,1:T(8,128)(2,1)S(1)}, u32[]{:S(2)}, u32[]{:S(2)}) collective-permute-start(bf16[128,4,128]{2,0,1:T(8,128)(2,1)} %get-tuple-element.3213), channel_id=1, source_target_pairs={{252,0},{0,4},{4,8},{8,12},{12,16},{16,20},{20,24},{24,28},{28,32}... | collective-permute-start | bytes 393224 | tf_op jit(solution)/shard_map/while/body/eval_jaxpr/ppermute | solution.py:24
  643.7 17.9 %collective-permute-start.13 = (bf16[128,4,128]{2,0,1:T(8,128)(2,1)}, bf16[128,4,128]{2,0,1:T(8,128)(2,1)S(1)}, u32[]{:S(2)}, u32[]{:S(2)}) collective-permute-start(bf16[128,4,128]{2,0,1:T(8,128)(2,1)} %get-tuple-element.3213), channel_id=1, source_target_pairs={{252,0},{0,4},{4,8},{8,12},{12,16},{16,20},{20,24},{24,28},{28,32}... | collective-permute-start | bytes 393224 | tf_op jit(solution)/shard_map/while/body/eval_jaxpr/ppermute | solution.py:24
  857.4 20.6 %collective-permute-start.21 = (bf16[256,4,128]{0,2,1:T(8,128)(2,1)S(1)}, bf16[256,4,128]{0,2,1:T(8,128)(2,1)}, u32[]{:S(2)}, u32[]{:S(2)}) collective-permute-start(bf16[256,4,128]{0,2,1:T(8,128)(2,1)S(1)} %copy.538), channel_id=1, source_target_pairs={{12,0},{16,4},{20,8},{24,12},{28,16},{32,20},{36,24},{40,28},{44,3... | collective-permute-start | bytes 786440 | tf_op jit(solution)/shard_map/ppermute | solution.py:24
  860.3 16.7 %collective-permute-start.22 = (bf16[128,4,128]{2,0,1:T(8,128)(2,1)S(1)}, bf16[128,4,128]{2,0,1:T(8,128)(2,1)S(1)}, u32[]{:S(2)}, u32[]{:S(2)}) collective-permute-start(bf16[128,4,128]{2,0,1:T(8,128)(2,1)S(1)} %copy-done.47), channel_id=1, source_target_pairs={{28,0},{32,4},{36,8},{40,12},{44,16},{48,20},{52,24},{56,28},{60,3... | collective-permute-start | bytes 393224 | tf_op jit(solution)/shard_map/ppermute | solution.py:24
  860.3 16.8 %collective-permute-start.19 = (bf16[128,4,128]{2,0,1:T(8,128)(2,1)S(1)}, bf16[128,4,128]{2,0,1:T(8,128)(2,1)S(1)}, u32[]{:S(2)}, u32[]{:S(2)}) collective-permute-start(bf16[128,4,128]{2,0,1:T(8,128)(2,1)S(1)} %copy-done.48), channel_id=1, source_target_pairs={{28,0},{32,4},{36,8},{40,12},{44,16},{48,20},{52,24},{56,28},{60,3... | collective-permute-start | bytes 393224 | tf_op jit(solution)/shard_map/ppermute | solution.py:24
  (241 other events, 6342.2 us)
